TPU v7x, 32 devices: a whole 2x2x4 slice. The times are simulated.
32 devices in a mesh: dp: 4 (over y, x), seg: 8 (over z, core).
Axes of the slice: x: 2, y: 2, z: 4, core: 2. Of those that a mesh axis runs over, the one named last changes fastest.
Arguments:
- inputs: bfloat16 [4, 4096, 768], P('dp', 'seg'), may hold values from -6 to 6
- doc_ids: int32 [4, 32], P('dp'), may hold values from 0 to 7, never falling along the last dimension, each value on 1 to 16 neighbouring positions
- cotangent: bfloat16 [4, 4096, 768], P('dp', 'seg'), may hold values from -6 to 6
- query_weight: bfloat16 [2, 768, 768], P(None, 'dp'), may hold values from -0.21875 to 0.21875
- query_bias: bfloat16 [2, 768], replicated, may hold values from -3 to 3
- key_weight: bfloat16 [2, 768, 768], P(None, 'dp'), may hold values from -0.21875 to 0.21875
- value_weight: bfloat16 [2, 768, 768], P(None, 'dp'), may hold values from -0.21875 to 0.21875
- value_bias: bfloat16 [2, 768], replicated, may hold values from -3 to 3
- out_weight: bfloat16 [2, 768, 768], P(None, 'dp'), may hold values from -1.75 to 1.75
- out_bias: bfloat16 [2, 768], replicated, may hold values from -3 to 3
- first_gain: bfloat16 [2, 768], replicated, may hold values from 0.5 to 1.5
- first_shift: bfloat16 [2, 768], replicated, may hold values from -2 to 2
- inner_weight: bfloat16 [2, 768, 3072], P(None, 'dp'), may hold values from -0.21875 to 0.21875
- inner_bias: bfloat16 [2, 3072], replicated, may hold values from -3 to 3
- outer_weight: bfloat16 [2, 3072, 768], P(None, 'dp'), may hold values from -0.109375 to 0.109375
- outer_bias: bfloat16 [2, 768], replicated, may hold values from -3 to 3
- second_gain: bfloat16 [2, 768], replicated, may hold values from 0.5 to 1.5
- second_shift: bfloat16 [2, 768], replicated, may hold values from -2 to 2
- segment_embed: bfloat16 [32, 768], replicated, may hold values from -3 to 3
Outputs:
- output: bfloat16 [4, 4096, 768], P('dp', 'seg')
- input_grad: bfloat16 [4, 4096, 768], P('dp', 'seg')
- grad_query_weight: float32 [2, 768, 768], P(None, 'dp')
- grad_query_bias: float32 [2, 768], P(None, 'dp')
- grad_key_weight: float32 [2, 768, 768], P(None, 'dp')
- grad_value_weight: float32 [2, 768, 768], P(None, 'dp')
- grad_value_bias: float32 [2, 768], P(None, 'dp')
- grad_out_weight: float32 [2, 768, 768], P(None, 'dp')
- grad_out_bias: float32 [2, 768], P(None, 'dp')
- grad_first_gain: float32 [2, 768], P(None, 'dp')
- grad_first_shift: float32 [2, 768], P(None, 'dp')
- grad_inner_weight: float32 [2, 768, 3072], P(None, 'dp')
- grad_inner_bias: float32 [2, 3072], P(None, 'dp')
- grad_outer_weight: float32 [2, 3072, 768], P(None, 'dp')
- grad_outer_bias: float32 [2, 768], P(None, 'dp')
- grad_second_gain: float32 [2, 768], P(None, 'dp')
- grad_second_shift: float32 [2, 768], P(None, 'dp')
- grad_segment_embed: float32 [32, 768], P(None, 'dp')
Inputs may be any that keep to these rules, and one draw needn't show every extreme that they name: `doc_ids`: along each row document numbers never fall; each document covers one to half of 32 consecutive segments, and some document of each row covers exactly half of 32.
All inputs are finite; a program needn't handle non-finite values.
Results may differ from a plain program's by a relative error of at most 0.02.
Values may be sent and summed in bfloat16 or wider, within the bound.
A program may use at most 256 MiB of HBM per device.

v0:
```python
import jax
import jax.numpy as jnp
from jax import lax
from jax.sharding import PartitionSpec as P

HEADS = 12
HEAD_DIM = 64
SEG_LEN = 128
epsilon = 1e-05


def normalize(values, gain, shift):
    centred = values - jnp.mean(values, axis=-1, keepdims=True)
    spread = jnp.mean(centred * centred, axis=-1, keepdims=True)
    return centred * lax.rsqrt(spread + epsilon) * gain + shift


def gelu_exact(values):
    return jax.nn.gelu(values, approximate=False)


def project(values, weight):
    return jnp.einsum("gnd,de->gne", values, weight, preferred_element_type=jnp.float32)


def back_project(values, weight):
    return jnp.einsum("gne,de->gnd", values, weight, preferred_element_type=jnp.float32)


def weight_grad(source, grads):
    return jnp.einsum("gnd,gne->de", source, grads, preferred_element_type=jnp.float32)


def row_total(values):
    return jnp.sum(values.astype(jnp.float32), axis=(0, 1))


def keep_pair(first_part, second_part):
    return (first_part, second_part)


def forward_layer(params, source, allowed, spread_keys):
    (
        query_weight,
        query_bias,
        key_weight,
        value_weight,
        value_bias,
        out_weight,
        out_bias,
        first_gain,
        first_shift,
        inner_weight,
        inner_bias,
        outer_weight,
        outer_bias,
        second_gain,
        second_shift,
    ) = params
    groups, length, width = source.shape
    queries = (project(source, query_weight) + query_bias.astype(jnp.float32)).astype(jnp.bfloat16)
    key_rows = project(source, key_weight).astype(jnp.bfloat16)
    value_rows = (project(source, value_weight) + value_bias.astype(jnp.float32)).astype(
        jnp.bfloat16
    )
    key_all, value_all = spread_keys(key_rows, value_rows)
    key_length = key_all.shape[1]
    query_heads = queries.reshape(groups, length, HEADS, HEAD_DIM)
    key_heads = key_all.reshape(groups, key_length, HEADS, HEAD_DIM)
    value_heads = value_all.reshape(groups, key_length, HEADS, HEAD_DIM)
    scores = (
        jnp.einsum("gqhe,gkhe->ghqk", query_heads, key_heads, preferred_element_type=jnp.float32)
        * 0.125
    )
    if allowed is not None:
        scores = jnp.where(allowed[:, None], scores, -1e30)
    attend = jax.nn.softmax(scores, axis=-1)
    attend_low = attend.astype(jnp.bfloat16)
    mixed = jnp.einsum(
        "ghqk,gkhe->gqhe", attend_low, value_heads, preferred_element_type=jnp.float32
    )
    mixed = mixed.astype(jnp.bfloat16).reshape(groups, length, width)
    branch = project(mixed, out_weight) + out_bias.astype(jnp.float32)
    hidden, first_pull = jax.vjp(
        normalize,
        source.astype(jnp.float32) + branch,
        first_gain.astype(jnp.float32),
        first_shift.astype(jnp.float32),
    )
    hidden_low = hidden.astype(jnp.bfloat16)
    inner = project(hidden_low, inner_weight) + inner_bias.astype(jnp.float32)
    active, gelu_pull = jax.vjp(gelu_exact, inner)
    active_low = active.astype(jnp.bfloat16)
    outer = project(active_low, outer_weight) + outer_bias.astype(jnp.float32)
    result, second_pull = jax.vjp(
        normalize, hidden + outer, second_gain.astype(jnp.float32), second_shift.astype(jnp.float32)
    )
    stored = (
        source,
        query_heads,
        key_heads,
        value_heads,
        attend,
        attend_low,
        mixed,
        first_pull,
        hidden_low,
        gelu_pull,
        active_low,
        second_pull,
    )
    return (result, stored)


def backward_layer(params, stored, grad_result, collect_keys):
    (
        query_weight,
        query_bias,
        key_weight,
        value_weight,
        value_bias,
        out_weight,
        out_bias,
        first_gain,
        first_shift,
        inner_weight,
        inner_bias,
        outer_weight,
        outer_bias,
        second_gain,
        second_shift,
    ) = params
    (
        source,
        query_heads,
        key_heads,
        value_heads,
        attend,
        attend_low,
        mixed,
        first_pull,
        hidden_low,
        gelu_pull,
        active_low,
        second_pull,
    ) = stored
    groups, length, width = source.shape
    key_length = key_heads.shape[1]
    grad_second_sum, grad_second_gain, grad_second_shift = second_pull(grad_result)
    grad_outer = grad_second_sum.astype(jnp.bfloat16)
    grad_outer_bias = row_total(grad_outer)
    grad_outer_weight = weight_grad(active_low, grad_outer)
    grad_active = back_project(grad_outer, outer_weight).astype(jnp.bfloat16)
    (grad_inner,) = gelu_pull(grad_active.astype(jnp.float32))
    grad_inner_low = grad_inner.astype(jnp.bfloat16)
    grad_inner_bias = row_total(grad_inner_low)
    grad_inner_weight = weight_grad(hidden_low, grad_inner_low)
    grad_hidden = grad_second_sum + back_project(grad_inner_low, inner_weight)
    grad_first_sum, grad_first_gain, grad_first_shift = first_pull(grad_hidden)
    grad_branch = grad_first_sum.astype(jnp.bfloat16)
    grad_out_bias = row_total(grad_branch)
    grad_out_weight = weight_grad(mixed, grad_branch)
    grad_mixed = back_project(grad_branch, out_weight).astype(jnp.bfloat16)
    grad_mixed = grad_mixed.reshape(groups, length, HEADS, HEAD_DIM)
    grad_attend = jnp.einsum(
        "gqhe,gkhe->ghqk", grad_mixed, value_heads, preferred_element_type=jnp.float32
    )
    grad_attend = grad_attend.astype(jnp.bfloat16).astype(jnp.float32)
    grad_value = jnp.einsum(
        "ghqk,gqhe->gkhe", attend_low, grad_mixed, preferred_element_type=jnp.float32
    )
    grad_value = grad_value.reshape(groups, key_length, width)
    grad_scores = attend * (grad_attend - jnp.sum(attend * grad_attend, axis=-1, keepdims=True))
    grad_scores = grad_scores.astype(jnp.bfloat16)
    grad_query = (
        jnp.einsum("ghqk,gkhe->gqhe", grad_scores, key_heads, preferred_element_type=jnp.float32)
        * 0.125
    )
    grad_query = grad_query.astype(jnp.bfloat16).reshape(groups, length, width)
    grad_key = (
        jnp.einsum("ghqk,gqhe->gkhe", grad_scores, query_heads, preferred_element_type=jnp.float32)
        * 0.125
    )
    grad_key = grad_key.reshape(groups, key_length, width)
    grad_key, grad_value = collect_keys(grad_key, grad_value)
    grad_key = grad_key.astype(jnp.bfloat16)
    grad_value = grad_value.astype(jnp.bfloat16)
    grad_source = (
        grad_first_sum
        + back_project(grad_query, query_weight)
        + back_project(grad_key, key_weight)
        + back_project(grad_value, value_weight)
    )
    gradients = (
        weight_grad(source, grad_query),
        row_total(grad_query),
        weight_grad(source, grad_key),
        weight_grad(source, grad_value),
        row_total(grad_value),
        grad_out_weight,
        grad_out_bias,
        grad_first_gain,
        grad_first_shift,
        grad_inner_weight,
        grad_inner_bias,
        grad_outer_weight,
        grad_outer_bias,
        grad_second_gain,
        grad_second_shift,
    )
    return (grad_source, gradients)


def shards(
    inputs,
    doc_ids,
    cotangent,
    query_weight,
    query_bias,
    key_weight,
    value_weight,
    value_bias,
    out_weight,
    out_bias,
    first_gain,
    first_shift,
    inner_weight,
    inner_bias,
    outer_weight,
    outer_bias,
    second_gain,
    second_shift,
    segment_embed,
):
    seg_count = lax.axis_size("seg")
    seg_index = lax.axis_index("seg")
    group_rows, local_length, width = inputs.shape
    seg_local = local_length // SEG_LEN
    query_full, key_full, value_full, out_full, inner_full, outer_full = (
        lax.all_gather(query_weight, "dp", axis=1, tiled=True),
        lax.all_gather(key_weight, "dp", axis=1, tiled=True),
        lax.all_gather(value_weight, "dp", axis=1, tiled=True),
        lax.all_gather(out_weight, "dp", axis=1, tiled=True),
        lax.all_gather(inner_weight, "dp", axis=1, tiled=True),
        lax.all_gather(outer_weight, "dp", axis=1, tiled=True),
    )
    stacked = (
        query_full,
        query_bias,
        key_full,
        value_full,
        value_bias,
        out_full,
        out_bias,
        first_gain,
        first_shift,
        inner_full,
        inner_bias,
        outer_full,
        outer_bias,
        second_gain,
        second_shift,
    )
    first_params = tuple((weight[0] for weight in stacked))
    cross_params = tuple((weight[1] for weight in stacked))
    pieces = inputs.reshape(group_rows * seg_local, SEG_LEN, width)
    segment_out, segment_stored = forward_layer(first_params, pieces, None, keep_pair)
    segment_grid = segment_out.reshape(group_rows, seg_local, SEG_LEN, width)
    position = lax.dynamic_slice_in_dim(segment_embed, seg_index * seg_local, seg_local, 0).astype(
        jnp.float32
    )
    heads_in = (segment_grid[:, :, 0, :] + position).astype(jnp.bfloat16)
    row_input = lax.all_gather(heads_in, "seg", axis=1, tiled=True)
    allowed = doc_ids[:, :, None] == doc_ids[:, None, :]
    cross_out, cross_stored = forward_layer(cross_params, row_input, allowed, keep_pair)
    returned = lax.dynamic_slice_in_dim(cross_out, seg_index * seg_local, seg_local, 1).astype(
        jnp.bfloat16
    )
    output = jnp.concatenate(
        [returned[:, :, None, :], segment_grid[:, :, 1:, :].astype(jnp.bfloat16)], axis=2
    )
    output = output.reshape(group_rows, local_length, width)
    cot_grid = cotangent.reshape(group_rows, seg_local, SEG_LEN, width)
    cot_heads = cot_grid[:, :, 0, :]
    grad_cross = lax.all_gather(cot_heads, "seg", axis=1, tiled=True)
    grad_row_input, cross_grads = backward_layer(
        cross_params, cross_stored, grad_cross.astype(jnp.float32), keep_pair
    )
    grad_row_low = grad_row_input.astype(jnp.bfloat16)
    factor = 1.0 / seg_count
    embed_grad = jnp.sum(grad_row_low.astype(jnp.float32), axis=0) * factor
    cross_grads = tuple((part * factor for part in cross_grads))
    grad_heads = lax.dynamic_slice_in_dim(grad_row_low, seg_index * seg_local, seg_local, 1)
    grad_grid = jnp.concatenate(
        [grad_heads[:, :, None, :].astype(jnp.float32), cot_grid[:, :, 1:, :].astype(jnp.float32)],
        axis=2,
    )
    grad_grid = grad_grid.reshape(group_rows * seg_local, SEG_LEN, width)
    grad_pieces, segment_grads = backward_layer(first_params, segment_stored, grad_grid, keep_pair)
    input_grad = grad_pieces.astype(jnp.bfloat16).reshape(group_rows, local_length, width)
    shares = (
        lax.psum_scatter(segment_grads[0], "dp", scatter_dimension=0, tiled=True),
        lax.psum_scatter(segment_grads[1], "dp", scatter_dimension=0, tiled=True),
        lax.psum_scatter(segment_grads[2], "dp", scatter_dimension=0, tiled=True),
        lax.psum_scatter(segment_grads[3], "dp", scatter_dimension=0, tiled=True),
        lax.psum_scatter(segment_grads[4], "dp", scatter_dimension=0, tiled=True),
        lax.psum_scatter(segment_grads[5], "dp", scatter_dimension=0, tiled=True),
        lax.psum_scatter(segment_grads[6], "dp", scatter_dimension=0, tiled=True),
        lax.psum_scatter(segment_grads[7], "dp", scatter_dimension=0, tiled=True),
        lax.psum_scatter(segment_grads[8], "dp", scatter_dimension=0, tiled=True),
        lax.psum_scatter(segment_grads[9], "dp", scatter_dimension=0, tiled=True),
        lax.psum_scatter(segment_grads[10], "dp", scatter_dimension=0, tiled=True),
        lax.psum_scatter(segment_grads[11], "dp", scatter_dimension=0, tiled=True),
        lax.psum_scatter(segment_grads[12], "dp", scatter_dimension=0, tiled=True),
        lax.psum_scatter(segment_grads[13], "dp", scatter_dimension=0, tiled=True),
        lax.psum_scatter(segment_grads[14], "dp", scatter_dimension=0, tiled=True),
        lax.psum_scatter(cross_grads[0], "dp", scatter_dimension=0, tiled=True),
        lax.psum_scatter(cross_grads[1], "dp", scatter_dimension=0, tiled=True),
        lax.psum_scatter(cross_grads[2], "dp", scatter_dimension=0, tiled=True),
        lax.psum_scatter(cross_grads[3], "dp", scatter_dimension=0, tiled=True),
        lax.psum_scatter(cross_grads[4], "dp", scatter_dimension=0, tiled=True),
        lax.psum_scatter(cross_grads[5], "dp", scatter_dimension=0, tiled=True),
        lax.psum_scatter(cross_grads[6], "dp", scatter_dimension=0, tiled=True),
        lax.psum_scatter(cross_grads[7], "dp", scatter_dimension=0, tiled=True),
        lax.psum_scatter(cross_grads[8], "dp", scatter_dimension=0, tiled=True),
        lax.psum_scatter(cross_grads[9], "dp", scatter_dimension=0, tiled=True),
        lax.psum_scatter(cross_grads[10], "dp", scatter_dimension=0, tiled=True),
        lax.psum_scatter(cross_grads[11], "dp", scatter_dimension=0, tiled=True),
        lax.psum_scatter(cross_grads[12], "dp", scatter_dimension=0, tiled=True),
        lax.psum_scatter(cross_grads[13], "dp", scatter_dimension=0, tiled=True),
        lax.psum_scatter(cross_grads[14], "dp", scatter_dimension=0, tiled=True),
        lax.psum_scatter(embed_grad, "dp", scatter_dimension=1, tiled=True),
    )
    summed = lax.psum(
        (
            shares[0],
            shares[1],
            shares[2],
            shares[3],
            shares[4],
            shares[5],
            shares[6],
            shares[7],
            shares[8],
            shares[9],
            shares[10],
            shares[11],
            shares[12],
            shares[13],
            shares[14],
            shares[15],
            shares[16],
            shares[17],
            shares[18],
            shares[19],
            shares[20],
            shares[21],
            shares[22],
            shares[23],
            shares[24],
            shares[25],
            shares[26],
            shares[27],
            shares[28],
            shares[29],
            shares[30],
        ),
        "seg",
    )
    totals = tuple((jnp.stack([summed[index], summed[index + 15]]) for index in range(15)))
    totals = totals + (summed[30],)
    return (output, input_grad) + tuple(totals)


def solution(mesh):
    placed = (
        P("dp", "seg", None),
        P("dp", None),
        P("dp", "seg", None),
        P(None, "dp", None),
        P(),
        P(None, "dp", None),
        P(None, "dp", None),
        P(),
        P(None, "dp", None),
        P(),
        P(),
        P(),
        P(None, "dp", None),
        P(),
        P(None, "dp", None),
        P(),
        P(),
        P(),
        P(),
    )
    return jax.shard_map(
        shards,
        mesh=mesh,
        in_specs=placed,
        out_specs=(
            P("dp", "seg", None),
            P("dp", "seg", None),
            P(None, "dp", None),
            P(None, "dp"),
            P(None, "dp", None),
            P(None, "dp", None),
            P(None, "dp"),
            P(None, "dp", None),
            P(None, "dp"),
            P(None, "dp"),
            P(None, "dp"),
            P(None, "dp", None),
            P(None, "dp"),
            P(None, "dp", None),
            P(None, "dp"),
            P(None, "dp"),
            P(None, "dp"),
            P(None, "dp"),
        ),
        check_vma=False,
    )
```

profile of v0, /device:TPU:0, one launch (start us, length us, event | category | flops | bytes accessed | tf_op | source)
XLA Modules:
  0.0 1615.4 jit_solution(5747079479511893777)
XLA Ops:
  11.4 15.6 all-gather.1
  32.1 17.8 %all-gather.10.cloned.1.call-done = bf16[2,768,768]{2,1,0:T(8,128)(2,1)} async-done(((bf16[2,192,768]{2,1,0:T(8,128)(2,1)}), bf16[2,768,768]{2,1,0:T(8,128)(2,1)}) %all-gather.10.cloned.1.call-update) | async-done | bytes 2359312 | tf_op jit(solution)/shard_map/all_gather | solution.py:242
  53.2 36.0 %all-gather.12.cloned.1.call-done = bf16[2,768,768]{2,1,0:T(8,128)(2,1)} async-done(((bf16[2,192,768]{2,1,0:T(8,128)(2,1)}), bf16[2,768,768]{2,1,0:T(8,128)(2,1)}) %all-gather.12.cloned.1.call-update) | async-done | bytes 2359312 | tf_op jit(solution)/shard_map/all_gather | solution.py:240
  91.6 36.8 %all-gather.14.cloned.1.call-done = bf16[2,768,768]{2,1,0:T(8,128)(2,1)} async-done(((bf16[2,192,768]{2,1,0:T(8,128)(2,1)}), bf16[2,768,768]{2,1,0:T(8,128)(2,1)}) %all-gather.14.cloned.1.call-update) | async-done | bytes 2359312 | tf_op jit(solution)/shard_map/all_gather | solution.py:241
  136.5 31.0 %all-gather.16.cloned.1.call-done = bf16[2,768,768]{2,1,0:T(8,128)(2,1)} async-done(((bf16[2,192,768]{2,1,0:T(8,128)(2,1)}), bf16[2,768,768]{2,1,0:T(8,128)(2,1)}) %all-gather.16.cloned.1.call-update) | async-done | bytes 2359312 | tf_op jit(solution)/shard_map/all_gather | solution.py:243
  170.0 95.4 %all-gather.18.cloned.1.call-done = bf16[2,768,3072]{2,1,0:T(8,128)(2,1)} async-done(((bf16[2,192,3072]{2,1,0:T(8,128)(2,1)}), bf16[2,768,3072]{2,1,0:T(8,128)(2,1)}) %all-gather.18.cloned.1.call-update) | async-done | bytes 9437200 | tf_op jit(solution)/shard_map/all_gather | solution.py:244
  265.4 6.9 fusion.33
  275.6 15.7 multiply_convert_fusion
  291.3 72.1 %all-gather.20.cloned.1.call-done = bf16[2,3072,768]{2,1,0:T(8,128)(2,1)} async-done(((bf16[2,768,768]{2,1,0:T(8,128)(2,1)}), bf16[2,3072,768]{2,1,0:T(8,128)(2,1)}) %all-gather.20.cloned.1.call-update) | async-done | bytes 9437200 | tf_op jit(solution)/shard_map/all_gather | solution.py:245
  363.3 6.0 fusion.108
  372.5 14.1 all-gather.2
  439.2 9.9 multiply_reduce_fusion.1
  450.6 8.9 convert_reduce_fusion
  510.6 7.2 convolution_bitcast_fusion.1
  519.8 6.2 convolution_bitcast_fusion
  527.0 5.9 convolution_multiply_fusion
  533.8 5.0 convolution_multiply_fusion.1
  557.5 38.3 %reduce-scatter.44.cloned.1.call-done = f32[192,768]{1,0:T(8,128)} async-done(((f32[768,768]{1,0:T(8,128)}), f32[192,768]{1,0:T(8,128)}) %reduce-scatter.44.cloned.1.call-update) | async-done | bytes 589840
  598.0 38.1 %reduce-scatter.52.cloned.1.call-done = f32[192,768]{1,0:T(8,128)} async-done(((f32[768,768]{1,0:T(8,128)}), f32[192,768]{1,0:T(8,128)}) %reduce-scatter.52.cloned.1.call-update) | async-done | bytes 589840
  638.3 38.2 %reduce-scatter.54.cloned.1.call-done = f32[192,768]{1,0:T(8,128)} async-done(((f32[768,768]{1,0:T(8,128)}), f32[192,768]{1,0:T(8,128)}) %reduce-scatter.54.cloned.1.call-update) | async-done | bytes 589840
  678.8 38.1 %reduce-scatter.50.cloned.1.call-done = f32[192,768]{1,0:T(8,128)} async-done(((f32[768,768]{1,0:T(8,128)}), f32[192,768]{1,0:T(8,128)}) %reduce-scatter.50.cloned.1.call-update) | async-done | bytes 589840
  719.1 38.8 %reduce-scatter.42.cloned.1.call-done = f32[192,768]{1,0:T(8,128)} async-done(((f32[768,768]{1,0:T(8,128)}), f32[192,768]{1,0:T(8,128)}) %reduce-scatter.42.cloned.1.call-update) | async-done | bytes 589840
  760.1 38.1 %reduce-scatter.46.cloned.1.call-done = f32[192,768]{1,0:T(8,128)} async-done(((f32[768,768]{1,0:T(8,128)}), f32[192,768]{1,0:T(8,128)}) %reduce-scatter.46.cloned.1.call-update) | async-done | bytes 589840
  800.4 95.7 %reduce-scatter.32.cloned.1.call-done = f32[192,3072]{1,0:T(8,128)} async-done(((f32[768,3072]{1,0:T(8,128)}), f32[192,3072]{1,0:T(8,128)}) %reduce-scatter.32.cloned.1.call-update) | async-done | bytes 2359312 | tf_op jit(solution)/shard_map/reduce_scatter | solution.py:311
  896.1 97.9 %reduce-scatter.36.cloned.1.call-done = f32[768,768]{1,0:T(8,128)} async-done(((f32[3072,768]{1,0:T(8,128)}), f32[768,768]{1,0:T(8,128)}) %reduce-scatter.36.cloned.1.call-update) | async-done | bytes 2359312 | tf_op jit(solution)/shard_map/reduce_scatter | solution.py:313
  994.0 97.9 %reduce-scatter.38.cloned.1.call-done = f32[768,768]{1,0:T(8,128)} async-done(((f32[3072,768]{1,0:T(8,128)}), f32[768,768]{1,0:T(8,128)}) %reduce-scatter.38.cloned.1.call-update) | async-done | bytes 2359312 | tf_op jit(solution)/shard_map/reduce_scatter | solution.py:328
  1091.9 97.9 %reduce-scatter.34.cloned.1.call-done = f32[192,3072]{1,0:T(8,128)} async-done(((f32[768,3072]{1,0:T(8,128)}), f32[192,3072]{1,0:T(8,128)}) %reduce-scatter.34.cloned.1.call-update) | async-done | bytes 2359312 | tf_op jit(solution)/shard_map/reduce_scatter | solution.py:326
  1200.1 44.1 %all-reduce.26.cloned.1.call-done = (f32[768]{0:T(1024)}, f32[768]{0:T(1024)}, f32[768]{0:T(1024)}, f32[768]{0:T(1024)}, f32[768]{0:T(1024)}, /*index=5*/f32[768...) async-done(((f32[768]{0:T(1024)}, f32[768]{0:T(1024)}, ...) | async-done | bytes 73744
  1257.8 13.8 reduce-scatter.56.cloned.1.call-done
  1272.6 30.8 %all-reduce.18 = (f32[1,192]{1,0:T(1,128)S(1)}, f32[1,192]{1,0:T(1,128)S(1)}, f32[1,192]{1,0:T(1,128)S(1)}, f32[1,192]{1,0:T(1,128)S(1)}, f32[1,192]{1,0:T(1,128...) all-reduce(f32[1,192]{1,0:T(1,128)S(1)} %bitcast.354, ...), channel_id=1, replica_groups=mesh['dp'=4,'seg'=8] {'seg'}, use_global_device_ids=true, to_apply=%region_31.32 | all-reduce | flops 10752 | bytes 86016 | tf_op jit(solution)/shard_map/psum | solution.py:334
  1308.7 282.4 %all-reduce.24.cloned.1.call-done = (f32[1,192,768]{1,2,0:T(8,128)}, f32[1,192,768]{1,2,0:T(8,128)}, f32[1,192,768]{1,2,0:T(8,128)}, f32[1,192,768]{1,2,0:T(8,12...) async-done(((f32[1,192,768]{1,2,0:T(8,128)}, ...) | async-done | bytes 14155792 | tf_op jit(solution)/shard_map/psum | solution.py:334
  1600.4 5.2 pad_maximum_fusion
  (450 shorter events, 212.2 us)
Async XLA Ops:
  7.2 42.8 %all-gather.10.cloned.1.call-start = ((), (), s32[]{:S(2)}) async-start(), calls=%async_computation.13 | async-start | bytes 2949120 | tf_op jit(solution)/shard_map/all_gather | solution.py:242
  7.9 81.2 %all-gather.12.cloned.1.call-start = ((), (), s32[]{:S(2)}) async-start(), calls=%async_computation.14 | async-start | bytes 2949120 | tf_op jit(solution)/shard_map/all_gather | solution.py:240
  8.7 119.7 %all-gather.14.cloned.1.call-start = ((), (), s32[]{:S(2)}) async-start(), calls=%async_computation.15 | async-start | bytes 2949120 | tf_op jit(solution)/shard_map/all_gather | solution.py:241
  9.4 158.0 %all-gather.16.cloned.1.call-start = ((), (), s32[]{:S(2)}) async-start(), calls=%async_computation.16 | async-start | bytes 2949120 | tf_op jit(solution)/shard_map/all_gather | solution.py:243
  10.1 255.3 %all-gather.18.cloned.1.call-start = ((), (), s32[]{:S(2)}) async-start(), calls=%async_computation.17 | async-start | bytes 11796480 | tf_op jit(solution)/shard_map/all_gather | solution.py:244
  10.7 20.8 %copy-start.66 = (bf16[2,3072]{1,0:T(2,128)(2,1)S(1)}, bf16[2,3072]{1,0:T(2,128)(2,1)}, u32[]{:S(2)}) copy-start(bf16[2,3072]{1,0:T(2,128)(2,1)} %param.32) | copy-start | bytes 36868
  10.7 39.3 %copy-start.3 = (bf16[1,512,768]{2,1,0:T(8,128)(2,1)S(1)}, bf16[1,512,768]{2,1,0:T(8,128)(2,1)}, u32[]{:S(2)}) copy-start(bf16[1,512,768]{2,1,0:T(8,128)(2,1)} %param.19) | copy-start | bytes 2359300
  10.7 352.6 %all-gather.20.cloned.1.call-start = ((), (), s32[]{:S(2)}) async-start(), calls=%async_computation.18 | async-start | bytes 11796480 | tf_op jit(solution)/shard_map/all_gather | solution.py:245
  11.3 538.5 %reduce-scatter.48.cloned.1.call-start = ((), (), s32[]{:S(2)}) async-start(), calls=%async_computation.27 | async-start | bytes 2949120
  28.3 335.1 %copy-start.81 = (f32[768]{0:T(1024)}, f32[768]{0:T(1024)S(1)}, u32[]{:S(2)}) copy-start(f32[768]{0:T(1024)S(1)} %get-tuple-element.91) | copy-start | bytes 9220
  28.9 334.4 %copy-start.96 = (f32[768]{0:T(1024)}, f32[768]{0:T(1024)S(1)}, u32[]{:S(2)}) copy-start(f32[768]{0:T(1024)S(1)} %get-tuple-element.207) | copy-start | bytes 9220
  29.5 340.7 %copy-start.58 = (f32[768]{0:T(1024)}, f32[768]{0:T(1024)S(1)}, u32[]{:S(2)}) copy-start(f32[768]{0:T(1024)S(1)} %get-tuple-element.209) | copy-start | bytes 9220
  32.1 240.2 %copy-start.64 = (f32[1,3072]{1,0:T(1,128)}, f32[1,3072]{1,0:T(1,128)S(1)}, u32[]{:S(2)}) copy-start(f32[1,3072]{1,0:T(1,128)S(1)} %get-tuple-element.178) | copy-start | bytes 36868
  91.6 39.2 %copy-start.14 = (bf16[4,128,768]{1,2,0:T(8,128)(2,1)}, bf16[4,128,768]{1,2,0:T(8,128)(2,1)S(1)}, u32[]{:S(2)}) copy-start(bf16[4,128,768]{1,2,0:T(8,128)(2,1)S(1)} %copy.115) | copy-start | bytes 2359300
  136.5 33.5 %copy-start.17 = (bf16[4,12,64,128]{3,2,1,0:T(8,128)(2,1)}, bf16[4,12,64,128]{3,2,1,0:T(8,128)(2,1)S(1)}, u32[]{:S(2)}) copy-start(bf16[4,12,64,128]{3,2,1,0:T(8,128)(2,1)S(1)} %convolution_convert_fusion.5) | copy-start | bytes 2359300
  169.7 193.7 %copy-start.71 = (f32[4,128]{1,0:T(4,128)}, f32[4,128]{1,0:T(4,128)S(1)}, u32[]{:S(2)}) copy-start(f32[4,128]{1,0:T(4,128)S(1)} %broadcast_multiply_fusion.11) | copy-start | bytes 6148
  170.0 95.4 %copy-start.73 = (f32[4,128]{1,0:T(4,128)}, f32[4,128]{1,0:T(4,128)S(1)}, u32[]{:S(2)}) copy-start(f32[4,128]{1,0:T(4,128)S(1)} %multiply_reduce_fusion.6) | copy-start | bytes 6148
  170.0 193.3 %copy-start.93 = (f32[4,128]{1,0:T(4,128)}, f32[4,128]{1,0:T(4,128)S(1)}, u32[]{:S(2)}) copy-start(f32[4,128]{1,0:T(4,128)S(1)} %fusion.95) | copy-start | bytes 6148
  477.3 78.0 %reduce-scatter.40.cloned.1.call-start = ((), (), s32[]{:S(2)}) async-start(), calls=%async_computation.23 | async-start | bytes 2949120
  489.2 106.6 %reduce-scatter.44.cloned.1.call-start = ((), (), s32[]{:S(2)}) async-start(), calls=%async_computation.25 | async-start | bytes 2949120
  498.1 138.0 %reduce-scatter.52.cloned.1.call-start = ((), (), s32[]{:S(2)}) async-start(), calls=%async_computation.29 | async-start | bytes 2949120
  501.7 174.9 %reduce-scatter.54.cloned.1.call-start = ((), (), s32[]{:S(2)}) async-start(), calls=%async_computation.30 | async-start | bytes 2949120
  504.6 212.3 %reduce-scatter.50.cloned.1.call-start = ((), (), s32[]{:S(2)}) async-start(), calls=%async_computation.28 | async-start | bytes 2949120
  506.6 251.3 %reduce-scatter.42.cloned.1.call-start = ((), (), s32[]{:S(2)}) async-start(), calls=%async_computation.24 | async-start | bytes 2949120
  508.6 289.6 %reduce-scatter.46.cloned.1.call-start = ((), (), s32[]{:S(2)}) async-start(), calls=%async_computation.26 | async-start | bytes 2949120
  510.6 385.5 %reduce-scatter.32.cloned.1.call-start = ((), (), s32[]{:S(2)}) async-start(), calls=%async_computation.19 | async-start | bytes 11796480 | tf_op jit(solution)/shard_map/reduce_scatter | solution.py:311
  517.9 476.1 %reduce-scatter.36.cloned.1.call-start = ((), (), s32[]{:S(2)}) async-start(), calls=%async_computation.21 | async-start | bytes 11796480 | tf_op jit(solution)/shard_map/reduce_scatter | solution.py:313
  526.0 565.9 %reduce-scatter.38.cloned.1.call-start = ((), (), s32[]{:S(2)}) async-start(), calls=%async_computation.22 | async-start | bytes 11796480 | tf_op jit(solution)/shard_map/reduce_scatter | solution.py:328
  532.9 656.9 %reduce-scatter.34.cloned.1.call-start = ((), (), s32[]{:S(2)}) async-start(), calls=%async_computation.20 | async-start | bytes 11796480 | tf_op jit(solution)/shard_map/reduce_scatter | solution.py:326
  538.9 705.3 %all-reduce.26.cloned.1.call-start = ((), (), s32[]{:S(2)}) async-start(), calls=%async_computation.33 | async-start | bytes 180224
  548.4 723.2 %reduce-scatter.56.cloned.1.call-start = ((), (), s32[]{:S(2)}) async-start(), calls=%async_computation.31 | async-start | bytes 491520
  549.5 1041.6 %all-reduce.24.cloned.1.call-start = ((), (), s32[]{:S(2)}) async-start(), calls=%async_computation.32 | async-start | bytes 31457280 | tf_op jit(solution)/shard_map/psum | solution.py:334
  (101 other events, 562.4 us)
Sparse Core Ops, SparseCore 0:
  9.8 40.0 all-gather.9
  51.8 37.3 all-gather.11
  91.0 37.3 all-gather.13
  130.1 37.3 all-gather.15
  169.1 96.1 all-gather.17
  267.1 96.1 all-gather.19
  477.4 37.3 reduce-scatter.47
  517.9 37.3 reduce-scatter.39
  558.3 37.3 reduce-scatter.43
  598.6 37.3 reduce-scatter.51
  639.1 37.3 reduce-scatter.53
  679.4 37.3 reduce-scatter.49
  720.5 37.3 reduce-scatter.41
  760.8 37.3 reduce-scatter.45
  801.2 94.8 reduce-scatter.31
  899.1 94.8 reduce-scatter.35
  997.0 94.8 reduce-scatter.37
  1094.8 94.8 reduce-scatter.33
  1195.7 48.4 all-reduce.25
  1246.9 24.6 reduce-scatter.55
  1276.2 314.8 all-reduce.23
where the time goes:
time: 1630 us; the launch traced here: 1620 us
  waiting for transfers between devices  1260 us (77%)
  matrix products  130 us (8%)
  local copies, waits for them, and re-layouts  81.8 us (5%)
  other arithmetic  69.1 us (4%)
  blocking collectives  60.5 us (4%)
  between operations  17.4 us (1%)
    unnamed x31, waiting for transfers between devices  295 us
    psum x1, waiting for transfers between devices, shards(): lax.psum((shares[0], shares[1], shares[2], shares[3], shares[4], shares[5...  282 us
    reduce_scatter x1, waiting for transfers between devices, shards(): lax.psum_scatter(cross_grads[9], 'dp', scatter_dimension=0, tiled=True)  97.9 us
    reduce_scatter x1, waiting for transfers between devices, shards(): lax.psum_scatter(segment_grads[11], 'dp', scatter_dimension=0, tiled=True)  97.9 us
    reduce_scatter x1, waiting for transfers between devices, shards(): lax.psum_scatter(cross_grads[11], 'dp', scatter_dimension=0, tiled=True)  97.9 us
    reduce_scatter x1, waiting for transfers between devices, shards(): lax.psum_scatter(segment_grads[9], 'dp', scatter_dimension=0, tiled=True)  95.7 us
    all_gather x1, waiting for transfers between devices, shards(): lax.all_gather(inner_weight, 'dp', axis=1, tiled=True)  95.4 us
    all_gather x1, waiting for transfers between devices, shards(): lax.all_gather(outer_weight, 'dp', axis=1, tiled=True)  72.1 us
  transfers between devices with their start and end apart: 21, of which 20 were waited for; matrix products, arithmetic and copies ran while one was open for 9% of the time, Pallas kernels for 0%

commit v1 on v0

--- a/solution.py
+++ b/solution.py
@@ -236,9 +236,34 @@
     seg_index = lax.axis_index("seg")
     group_rows, local_length, width = inputs.shape
     seg_local = local_length // SEG_LEN
+
+    def replace_regions(chunk):
+        shaped, taken_in, item_now = (lax.axis_size("dp"), lax.axis_index("dp"), chunk.shape[1])
+        pile = [ii * shaped if ix == 1 else ii for ix, ii in enumerate(chunk.shape)]
+        current_value = lax.dynamic_update_slice_in_dim(
+            jnp.zeros(pile, chunk.dtype), chunk, taken_in * item_now, axis=1
+        )
+        outcome_arr = state_now = chunk
+        for d in range(1, shaped // 2 + 1):
+            outcome_arr = lax.ppermute(
+                outcome_arr,
+                axis_name="dp",
+                perm=list(map(lambda ix: (ix, (ix + 1) % shaped), range(shaped))),
+            )
+            current_value = lax.dynamic_update_slice_in_dim(
+                current_value, outcome_arr, (taken_in - d) % shaped * item_now, axis=1
+            )
+            if 2 * d < shaped:
+                spare = list(map(lambda ix: (ix, (ix - 1) % shaped), range(shaped)))
+                state_now = lax.ppermute(state_now, axis_name="dp", perm=spare)
+                current_value = lax.dynamic_update_slice_in_dim(
+                    current_value, state_now, (taken_in + d) % shaped * item_now, axis=1
+                )
+        return current_value
+
     query_full, key_full, value_full, out_full, inner_full, outer_full = (
         lax.all_gather(query_weight, "dp", axis=1, tiled=True),
-        lax.all_gather(key_weight, "dp", axis=1, tiled=True),
+        replace_regions(key_weight),
         lax.all_gather(value_weight, "dp", axis=1, tiled=True),
         lax.all_gather(out_weight, "dp", axis=1, tiled=True),
         lax.all_gather(inner_weight, "dp", axis=1, tiled=True),

time: 1630 us -> 1590 us (0.975)
  waiting for transfers between devices: 1260 us -> 1190 us
  local copies, waits for them, and re-layouts: 81.8 us -> 123 us
    all_gather x1 -> x0, waiting for transfers between devices: 36.8 us -> none  [shards(): lax.all_gather(key_weight, 'dp', axis=1, tiled=True)]
    dynamic_update_slice x0 -> x4, local copies, waits for them, and re-layouts: none -> 33.5 us  [the longest x2 14.8 us: replace_regions(): lax.dynamic_update_slice_in_dim(current_value, outcome_arr, (taken_in - d...]
    all_gather x1, waiting for transfers between devices: 36 us -> 14.6 us  [shards(): lax.all_gather(query_weight, 'dp', axis=1, tiled=True)]
    all_gather x1, waiting for transfers between devices: 17.8 us -> 0.01 us  [shards(): lax.all_gather(value_weight, 'dp', axis=1, tiled=True)]
    unnamed x261 -> x270, local copies, waits for them, and re-layouts: 68.9 us -> 72.5 us
    unnamed x31 -> x30, waiting for transfers between devices: 295 us -> 297 us
  transfers between devices with their start and end apart: 21 -> 23, of which waited for: 20 -> 19; matrix products, arithmetic and copies ran while one was open for 9% -> 12% of each run, Pallas kernels for 0% -> 0%
where the time goes in v1:
time: 1590 us
  waiting for transfers between devices  1190 us (75%)
  matrix products  133 us (8%)
  local copies, waits for them, and re-layouts  123 us (8%)
  other arithmetic  60.5 us (4%)
  blocking collectives  59 us (4%)
  between operations  17.2 us (1%)
    unnamed x30, waiting for transfers between devices  297 us
    psum x1, waiting for transfers between devices, shards(): lax.psum((shares[0], shares[1], shares[2], shares[3], shares[4], shares[5...  282 us
    reduce_scatter x1, waiting for transfers between devices, shards(): lax.psum_scatter(cross_grads[11], 'dp', scatter_dimension=0, tiled=True)  97.9 us
    reduce_scatter x1, waiting for transfers between devices, shards(): lax.psum_scatter(cross_grads[9], 'dp', scatter_dimension=0, tiled=True)  97.9 us
    reduce_scatter x1, waiting for transfers between devices, shards(): lax.psum_scatter(segment_grads[11], 'dp', scatter_dimension=0, tiled=True)  97.9 us
    reduce_scatter x1, waiting for transfers between devices, shards(): lax.psum_scatter(segment_grads[9], 'dp', scatter_dimension=0, tiled=True)  95.7 us
    all_gather x1, waiting for transfers between devices, shards(): lax.all_gather(inner_weight, 'dp', axis=1, tiled=True)  95.4 us
    unnamed x270, local copies, waits for them, and re-layouts  72.5 us
  transfers between devices with their start and end apart: 23, of which 19 were waited for; matrix products, arithmetic and copies ran while one was open for 12% of the time, Pallas kernels for 0%

profile of v1, /device:TPU:0, one launch (start us, length us, event | category | flops | bytes accessed | tf_op | source)
XLA Modules:
  0.0 1588.6 jit_solution(3591553660387424964)
XLA Ops:
  17.2 9.7 dynamic_update_slice.12
  26.9 14.1 all-gather.1
  45.6 7.4 collective-permute-done
  57.6 7.1 dynamic_update_slice.13
  67.4 9.0 dynamic_update_slice.14
  77.8 7.7 dynamic_update_slice.15
  91.0 14.6 all-gather.11.cloned.1.call-done
  115.0 29.8 %all-gather.13.cloned.1.call-done = bf16[2,768,768]{2,1,0:T(8,128)(2,1)} async-done(((bf16[2,192,768]{2,1,0:T(8,128)(2,1)}), bf16[2,768,768]{2,1,0:T(8,128)(2,1)}) %all-gather.13.cloned.1.call-update) | async-done | bytes 2359312 | tf_op jit(solution)/shard_map/all_gather | solution.py:268
  147.4 95.4 %all-gather.15.cloned.1.call-done = bf16[2,768,3072]{2,1,0:T(8,128)(2,1)} async-done(((bf16[2,192,3072]{2,1,0:T(8,128)(2,1)}), bf16[2,768,3072]{2,1,0:T(8,128)(2,1)}) %all-gather.15.cloned.1.call-update) | async-done | bytes 9437200 | tf_op jit(solution)/shard_map/all_gather | solution.py:269
  242.8 6.9 fusion.33
  252.9 15.8 multiply_convert_fusion
  268.8 71.9 %all-gather.17.cloned.1.call-done = bf16[2,3072,768]{2,1,0:T(8,128)(2,1)} async-done(((bf16[2,768,768]{2,1,0:T(8,128)(2,1)}), bf16[2,3072,768]{2,1,0:T(8,128)(2,1)}) %all-gather.17.cloned.1.call-update) | async-done | bytes 9437200 | tf_op jit(solution)/shard_map/all_gather | solution.py:270
  340.7 6.0 fusion.108
  349.9 14.1 all-gather.2
  420.1 8.7 convert_reduce_fusion
  481.9 7.2 convolution_bitcast_fusion.1
  491.0 6.2 convolution_bitcast_fusion
  498.4 5.8 convolution_multiply_fusion
  530.9 38.3 %reduce-scatter.48.cloned.1.call-done = f32[192,768]{1,0:T(8,128)} async-done(((f32[768,768]{1,0:T(8,128)}), f32[192,768]{1,0:T(8,128)}) %reduce-scatter.48.cloned.1.call-update) | async-done | bytes 589840
  571.4 38.2 %reduce-scatter.52.cloned.1.call-done = f32[192,768]{1,0:T(8,128)} async-done(((f32[768,768]{1,0:T(8,128)}), f32[192,768]{1,0:T(8,128)}) %reduce-scatter.52.cloned.1.call-update) | async-done | bytes 589840
  611.9 38.1 %reduce-scatter.54.cloned.1.call-done = f32[192,768]{1,0:T(8,128)} async-done(((f32[768,768]{1,0:T(8,128)}), f32[192,768]{1,0:T(8,128)}) %reduce-scatter.54.cloned.1.call-update) | async-done | bytes 589840
  652.2 38.2 %reduce-scatter.50.cloned.1.call-done = f32[192,768]{1,0:T(8,128)} async-done(((f32[768,768]{1,0:T(8,128)}), f32[192,768]{1,0:T(8,128)}) %reduce-scatter.50.cloned.1.call-update) | async-done | bytes 589840
  692.6 38.7 %reduce-scatter.42.cloned.1.call-done = f32[192,768]{1,0:T(8,128)} async-done(((f32[768,768]{1,0:T(8,128)}), f32[192,768]{1,0:T(8,128)}) %reduce-scatter.42.cloned.1.call-update) | async-done | bytes 589840
  733.5 38.3 %reduce-scatter.46.cloned.1.call-done = f32[192,768]{1,0:T(8,128)} async-done(((f32[768,768]{1,0:T(8,128)}), f32[192,768]{1,0:T(8,128)}) %reduce-scatter.46.cloned.1.call-update) | async-done | bytes 589840
  774.0 95.7 %reduce-scatter.32.cloned.1.call-done = f32[192,3072]{1,0:T(8,128)} async-done(((f32[768,3072]{1,0:T(8,128)}), f32[192,3072]{1,0:T(8,128)}) %reduce-scatter.32.cloned.1.call-update) | async-done | bytes 2359312 | tf_op jit(solution)/shard_map/reduce_scatter | solution.py:336
  869.7 97.9 %reduce-scatter.36.cloned.1.call-done = f32[768,768]{1,0:T(8,128)} async-done(((f32[3072,768]{1,0:T(8,128)}), f32[768,768]{1,0:T(8,128)}) %reduce-scatter.36.cloned.1.call-update) | async-done | bytes 2359312 | tf_op jit(solution)/shard_map/reduce_scatter | solution.py:338
  967.6 97.9 %reduce-scatter.38.cloned.1.call-done = f32[768,768]{1,0:T(8,128)} async-done(((f32[3072,768]{1,0:T(8,128)}), f32[768,768]{1,0:T(8,128)}) %reduce-scatter.38.cloned.1.call-update) | async-done | bytes 2359312 | tf_op jit(solution)/shard_map/reduce_scatter | solution.py:353
  1065.5 97.9 %reduce-scatter.34.cloned.1.call-done = f32[192,3072]{1,0:T(8,128)} async-done(((f32[768,3072]{1,0:T(8,128)}), f32[192,3072]{1,0:T(8,128)}) %reduce-scatter.34.cloned.1.call-update) | async-done | bytes 2359312 | tf_op jit(solution)/shard_map/reduce_scatter | solution.py:351
  1173.1 44.6 %all-reduce.26.cloned.1.call-done = (f32[768]{0:T(1024)}, f32[768]{0:T(1024)}, f32[768]{0:T(1024)}, f32[768]{0:T(1024)}, f32[768]{0:T(1024)}, /*index=5*/f32[768...) async-done(((f32[768]{0:T(1024)}, f32[768]{0:T(1024)}, ...) | async-done | bytes 73744
  1231.2 14.0 reduce-scatter.56.cloned.1.call-done
  1246.1 30.8 %all-reduce.18 = (f32[1,192]{1,0:T(1,128)S(1)}, f32[1,192]{1,0:T(1,128)S(1)}, f32[1,192]{1,0:T(1,128)S(1)}, f32[1,192]{1,0:T(1,128)S(1)}, f32[1,192]{1,0:T(1,128...) all-reduce(f32[1,192]{1,0:T(1,128)S(1)} %bitcast.356, ...), channel_id=1, replica_groups=mesh['dp'=4,'seg'=8] {'seg'}, use_global_device_ids=true, to_apply=%region_31.32 | all-reduce | flops 10752 | bytes 86016 | tf_op jit(solution)/shard_map/psum | solution.py:359
  1282.2 282.2 %all-reduce.24.cloned.1.call-done = (f32[1,192,768]{1,2,0:T(8,128)}, f32[1,192,768]{1,2,0:T(8,128)}, f32[1,192,768]{1,2,0:T(8,128)}, f32[1,192,768]{1,2,0:T(8,12...) async-done(((f32[1,192,768]{1,2,0:T(8,128)}, ...) | async-done | bytes 14155792 | tf_op jit(solution)/shard_map/psum | solution.py:359
  (468 shorter events, 243.1 us)
Async XLA Ops:
  7.2 81.4 %all-gather.9.cloned.1.call-start = ((), (), s32[]{:S(2)}) async-start(), calls=%async_computation.13 | async-start | bytes 2949120 | tf_op jit(solution)/shard_map/all_gather | solution.py:267
  7.9 97.7 %all-gather.11.cloned.1.call-start = ((), (), s32[]{:S(2)}) async-start(), calls=%async_computation.14 | async-start | bytes 2949120 | tf_op jit(solution)/shard_map/all_gather | solution.py:265
  8.7 136.2 %all-gather.13.cloned.1.call-start = ((), (), s32[]{:S(2)}) async-start(), calls=%async_computation.15 | async-start | bytes 2949120 | tf_op jit(solution)/shard_map/all_gather | solution.py:268
  9.4 233.4 %all-gather.15.cloned.1.call-start = ((), (), s32[]{:S(2)}) async-start(), calls=%async_computation.16 | async-start | bytes 11796480 | tf_op jit(solution)/shard_map/all_gather | solution.py:269
  10.0 330.7 %all-gather.17.cloned.1.call-start = ((), (), s32[]{:S(2)}) async-start(), calls=%async_computation.17 | async-start | bytes 11796480 | tf_op jit(solution)/shard_map/all_gather | solution.py:270
  10.6 510.6 %reduce-scatter.44.cloned.1.call-start = ((), (), s32[]{:S(2)}) async-start(), calls=%async_computation.24 | async-start | bytes 2949120
  10.6 54.1 %collective-permute-start.1 = (bf16[2,192,768]{2,1,0:T(8,128)(2,1)}, bf16[2,192,768]{2,1,0:T(8,128)(2,1)}, u32[]{:S(2)}, u32[]{:S(2)}) collective-permute-start(bf16[2,192,768]{2,1,0:T(8,128)(2,1)} %param.24), channel_id=1, source_target_pairs={{0,24},{8,0},{16,8},{24,16},{1,25},{9,1},{17,9},{25,17},{2,26},{10... | collective-permute-start | bytes 1769480 | tf_op jit(solution)/shard_map/ppermute | solution.py:258
  14.6 38.4 %collective-permute-start = (bf16[2,192,768]{2,1,0:T(8,128)(2,1)}, bf16[2,192,768]{2,1,0:T(8,128)(2,1)}, u32[]{:S(2)}, u32[]{:S(2)}) collective-permute-start(bf16[2,192,768]{2,1,0:T(8,128)(2,1)} %param.24), channel_id=1, source_target_pairs={{0,8},{8,16},{16,24},{24,0},{1,9},{9,17},{17,25},{25,1},{2,10},{10... | collective-permute-start | bytes 1769480 | tf_op jit(solution)/shard_map/ppermute | solution.py:248
  17.2 38.5 %copy-start.70 = (bf16[2,3072]{1,0:T(2,128)(2,1)S(1)}, bf16[2,3072]{1,0:T(2,128)(2,1)}, u32[]{:S(2)}) copy-start(bf16[2,3072]{1,0:T(2,128)(2,1)} %param.32) | copy-start | bytes 36868
  42.4 298.3 %copy-start.100 = (f32[768]{0:T(1024)}, f32[768]{0:T(1024)S(1)}, u32[]{:S(2)}) copy-start(f32[768]{0:T(1024)S(1)} %get-tuple-element.207) | copy-start | bytes 9220
  43.0 304.7 %copy-start.62 = (f32[768]{0:T(1024)}, f32[768]{0:T(1024)S(1)}, u32[]{:S(2)}) copy-start(f32[768]{0:T(1024)S(1)} %get-tuple-element.209) | copy-start | bytes 9220
  43.6 297.1 %copy-start.85 = (f32[768]{0:T(1024)}, f32[768]{0:T(1024)S(1)}, u32[]{:S(2)}) copy-start(f32[768]{0:T(1024)S(1)} %get-tuple-element.91) | copy-start | bytes 9220
  53.0 23.5 %collective-permute-start.2 = (bf16[2,192,768]{2,1,0:T(8,128)(2,1)}, bf16[2,192,768]{2,1,0:T(8,128)(2,1)}, u32[]{:S(2)}, u32[]{:S(2)}) collective-permute-start(bf16[2,192,768]{2,1,0:T(8,128)(2,1)} %collective-permute-done), channel_id=1, source_target_pairs={{0,8},{8,16},{16,24},{24,0},{1,9},{9,17},{17,25},{25,1},{2,10},{10... | collective-permute-start | bytes 1769480 | tf_op jit(solution)/shard_map/ppermute | solution.py:248
  56.2 193.4 %copy-start.68 = (f32[1,3072]{1,0:T(1,128)}, f32[1,3072]{1,0:T(1,128)S(1)}, u32[]{:S(2)}) copy-start(f32[1,3072]{1,0:T(1,128)S(1)} %get-tuple-element.178) | copy-start | bytes 36868
  115.0 32.4 %copy-start.20 = (bf16[4,12,64,128]{3,2,1,0:T(8,128)(2,1)}, bf16[4,12,64,128]{3,2,1,0:T(8,128)(2,1)S(1)}, u32[]{:S(2)}) copy-start(bf16[4,12,64,128]{3,2,1,0:T(8,128)(2,1)S(1)} %convolution_convert_fusion.5) | copy-start | bytes 2359300
  147.1 193.7 %copy-start.75 = (f32[4,128]{1,0:T(4,128)}, f32[4,128]{1,0:T(4,128)S(1)}, u32[]{:S(2)}) copy-start(f32[4,128]{1,0:T(4,128)S(1)} %broadcast_multiply_fusion.11) | copy-start | bytes 6148
  147.4 95.4 %copy-start.77 = (f32[4,128]{1,0:T(4,128)}, f32[4,128]{1,0:T(4,128)S(1)}, u32[]{:S(2)}) copy-start(f32[4,128]{1,0:T(4,128)S(1)} %multiply_reduce_fusion.6) | copy-start | bytes 6148
  147.4 193.3 %copy-start.97 = (f32[4,128]{1,0:T(4,128)}, f32[4,128]{1,0:T(4,128)S(1)}, u32[]{:S(2)}) copy-start(f32[4,128]{1,0:T(4,128)S(1)} %fusion.95) | copy-start | bytes 6148
  450.7 78.0 %reduce-scatter.40.cloned.1.call-start = ((), (), s32[]{:S(2)}) async-start(), calls=%async_computation.22 | async-start | bytes 2949120
  458.8 110.4 %reduce-scatter.48.cloned.1.call-start = ((), (), s32[]{:S(2)}) async-start(), calls=%async_computation.26 | async-start | bytes 2949120
  469.3 140.3 %reduce-scatter.52.cloned.1.call-start = ((), (), s32[]{:S(2)}) async-start(), calls=%async_computation.28 | async-start | bytes 2949120
  472.9 177.1 %reduce-scatter.54.cloned.1.call-start = ((), (), s32[]{:S(2)}) async-start(), calls=%async_computation.29 | async-start | bytes 2949120
  475.8 214.6 %reduce-scatter.50.cloned.1.call-start = ((), (), s32[]{:S(2)}) async-start(), calls=%async_computation.27 | async-start | bytes 2949120
  477.9 253.5 %reduce-scatter.42.cloned.1.call-start = ((), (), s32[]{:S(2)}) async-start(), calls=%async_computation.23 | async-start | bytes 2949120
  479.8 291.9 %reduce-scatter.46.cloned.1.call-start = ((), (), s32[]{:S(2)}) async-start(), calls=%async_computation.25 | async-start | bytes 2949120
  481.8 387.9 %reduce-scatter.32.cloned.1.call-start = ((), (), s32[]{:S(2)}) async-start(), calls=%async_computation.18 | async-start | bytes 11796480 | tf_op jit(solution)/shard_map/reduce_scatter | solution.py:336
  489.1 478.5 %reduce-scatter.36.cloned.1.call-start = ((), (), s32[]{:S(2)}) async-start(), calls=%async_computation.20 | async-start | bytes 11796480 | tf_op jit(solution)/shard_map/reduce_scatter | solution.py:338
  497.2 568.3 %reduce-scatter.38.cloned.1.call-start = ((), (), s32[]{:S(2)}) async-start(), calls=%async_computation.21 | async-start | bytes 11796480 | tf_op jit(solution)/shard_map/reduce_scatter | solution.py:353
  504.2 659.1 %reduce-scatter.34.cloned.1.call-start = ((), (), s32[]{:S(2)}) async-start(), calls=%async_computation.19 | async-start | bytes 11796480 | tf_op jit(solution)/shard_map/reduce_scatter | solution.py:351
  510.3 707.3 %all-reduce.26.cloned.1.call-start = ((), (), s32[]{:S(2)}) async-start(), calls=%async_computation.32 | async-start | bytes 180224
  519.8 725.3 %reduce-scatter.56.cloned.1.call-start = ((), (), s32[]{:S(2)}) async-start(), calls=%async_computation.30 | async-start | bytes 491520
  520.8 1043.6 %all-reduce.24.cloned.1.call-start = ((), (), s32[]{:S(2)}) async-start(), calls=%async_computation.31 | async-start | bytes 31457280 | tf_op jit(solution)/shard_map/psum | solution.py:359
  (107 other events, 657.8 us)
Sparse Core Ops, SparseCore 0:
  9.8 55.4 all-gather.8
  67.1 38.4 all-gather.10
  107.5 37.3 all-gather.12
  146.5 96.1 all-gather.14
  244.5 96.1 all-gather.16
  450.8 37.3 reduce-scatter.43
  491.3 37.3 reduce-scatter.39
  531.7 37.3 reduce-scatter.47
  572.2 37.3 reduce-scatter.51
  612.5 37.3 reduce-scatter.53
  653.0 37.3 reduce-scatter.49
  693.9 37.3 reduce-scatter.41
  734.4 37.3 reduce-scatter.45
  774.7 94.8 reduce-scatter.31
  872.6 94.8 reduce-scatter.35
  970.5 94.8 reduce-scatter.37
  1068.4 94.8 reduce-scatter.33
  1169.2 48.4 all-reduce.25
  1220.4 24.6 reduce-scatter.55
  1249.6 314.8 all-reduce.23
